TPU v7x, 32 devices: a whole 2x2x4 slice. The times are simulated.
32 devices in a mesh: dp: 8 (over y, x, core), mp: 4 (over z).
Axes of the slice: x: 2, y: 2, z: 4, core: 2. Of those that a mesh axis runs over, the one named last changes fastest.
Arguments:
- latents: float32 [3, 8192, 1024], P(None, ('dp', 'mp')), may hold values from -6 to 6
- group_ids: int32 [3, 8, 1024], P(None, 'dp'), may hold values from 0 to 15, never falling along the last dimension, each value on 1 to 128 neighbouring positions
- pad_mask: int32 [3, 8, 1024], P(None, 'dp'), may hold values 0 or 1
- w_qkv: bfloat16 [3, 1024, 1024], P(None, 'dp', 'mp'), may hold values from -0.1875 to 0.1875
- w_out: bfloat16 [1024, 1024], P('dp', 'mp'), may hold values from -0.5 to 0.5
- w_up: bfloat16 [1024, 4096], P('dp', 'mp'), may hold values from -0.1875 to 0.1875
- w_down: bfloat16 [1024, 4096], P('dp', 'mp'), may hold values from -0.09375 to 0.09375
- norm_gain: bfloat16 [2, 1024], P(None, 'dp'), may hold values from 0.099609375 to 1.8984375
- norm_bias: bfloat16 [2, 1024], P(None, 'dp'), may hold values from -3 to 3
- out_grad: float32 [3, 8192, 1024], P(None, ('dp', 'mp')), may hold values from -6 to 6
Outputs:
- latents_out: float32 [3, 8192, 1024], P(None, ('dp', 'mp'))
- latents_grad: float32 [3, 8192, 1024], P(None, ('dp', 'mp'))
- grad_qkv: float32 [3, 1024, 1024], P(None, 'dp', 'mp')
- grad_out: float32 [1024, 1024], P('dp', 'mp')
- grad_up: float32 [1024, 4096], P('dp', 'mp')
- grad_down: float32 [1024, 4096], P('dp', 'mp')
- grad_gain: float32 [2, 1024], P(None, 'dp')
- grad_bias: float32 [2, 1024], P(None, 'dp')
Inputs may be any that keep to these rules, and one draw needn't show every extreme that they name: `group_ids`: group numbers along one clip never fall; each group of a clip holds 1 to 128 latents and one holds exactly 128.
All inputs are finite; a program needn't handle non-finite values. No bound on the sum of `pad_mask` on one device may be relied on, other than what follows from the above.
Results may differ from a plain program's by a relative error of at most 0.0095.
Values may be sent and summed in bfloat16 or wider, within the bound.
No kernel may reach another device: no remote copies, remote signals or barrier semaphores. Data moves between devices by JAX's collectives and lax.ppermute only.
A program may use at most 192 MiB of HBM per device.

v0:
```python
import jax
import jax.numpy as jnp
from jax import lax
from jax.sharding import PartitionSpec as P

HEAD_DIM = 128
epsilon = 1e-05


def norm_rows(values, scaling, offset):
    row_mean = jnp.mean(values, axis=-1, keepdims=True)
    centred = values - row_mean
    row_var = jnp.mean(centred * centred, axis=-1, keepdims=True)
    return centred * lax.rsqrt(row_var + epsilon) * scaling + offset


def spread_rows(rows_local):
    return lax.all_gather(rows_local, "mp", axis=0, tiled=True)


def settle_rows(partial_rows):
    return lax.psum_scatter(partial_rows, "mp", scatter_dimension=0, tiled=True)


def block_mask(group_row, live_row, first_row, block_rows):
    positions = jnp.arange(group_row.shape[0], dtype=jnp.int32)
    query_positions = first_row + jnp.arange(block_rows, dtype=jnp.int32)
    query_groups = lax.dynamic_slice_in_dim(group_row, first_row, block_rows)
    same_group = query_groups[:, None] == group_row[None, :]
    return same_group & (
        (live_row[None, :] == 1) | (query_positions[:, None] == positions[None, :])
    )


def block_scores(query_block, keys, allowed, factor):
    scores = (
        jnp.einsum("qhd,khd->hqk", query_block, keys, preferred_element_type=jnp.float32) * factor
    )
    return jnp.where(allowed[None], scores, -1e30)


def attend_forward(queries, keys, values, group_row, live_row, block_rows, factor):
    seq_len = keys.shape[0]
    block_count = seq_len // block_rows

    def one_block(block_index):
        first_row = block_index * block_rows
        query_block = lax.dynamic_slice_in_dim(queries, first_row, block_rows, 0)
        scores = block_scores(
            query_block, keys, block_mask(group_row, live_row, first_row, block_rows), factor
        )
        row_peak = jnp.max(scores, axis=-1, keepdims=True)
        weights = jnp.exp(scores - row_peak)
        totals = jnp.sum(weights, axis=-1, keepdims=True)
        probabilities = (weights / totals).astype(jnp.bfloat16)
        mixture = jnp.einsum(
            "hqk,khd->qhd", probabilities, values, preferred_element_type=jnp.float32
        )
        return (mixture, (row_peak + jnp.log(totals))[..., 0])

    mixture, log_totals = lax.map(one_block, jnp.arange(block_count, dtype=jnp.int32))
    return (mixture.reshape(seq_len, mixture.shape[2], mixture.shape[3]), log_totals)


def attend_backward(
    queries, keys, values, grad_mix, log_totals, group_row, live_row, block_rows, factor
):
    seq_len = keys.shape[0]
    block_count = seq_len // block_rows

    def one_block(carry, block_index):
        grad_keys, grad_values = carry
        first_row = block_index * block_rows
        query_block = lax.dynamic_slice_in_dim(queries, first_row, block_rows, 0)
        grad_block = lax.dynamic_slice_in_dim(grad_mix, first_row, block_rows, 0)
        scores = block_scores(
            query_block, keys, block_mask(group_row, live_row, first_row, block_rows), factor
        )
        probabilities = jnp.exp(scores - log_totals[block_index][:, :, None])
        grad_probs = jnp.einsum(
            "qhd,khd->hqk", grad_block, values, preferred_element_type=jnp.float32
        )
        weighted = jnp.sum(probabilities * grad_probs, axis=-1, keepdims=True)
        grad_scores = (probabilities * (grad_probs - weighted)).astype(jnp.bfloat16)
        grad_query = (
            jnp.einsum("hqk,khd->qhd", grad_scores, keys, preferred_element_type=jnp.float32)
            * factor
        )
        grad_keys = (
            grad_keys
            + jnp.einsum(
                "hqk,qhd->khd", grad_scores, query_block, preferred_element_type=jnp.float32
            )
            * factor
        )
        grad_values = grad_values + jnp.einsum(
            "hqk,qhd->khd",
            probabilities.astype(jnp.bfloat16),
            grad_block,
            preferred_element_type=jnp.float32,
        )
        return ((grad_keys, grad_values), grad_query)

    zeros_kv = jnp.zeros(keys.shape, jnp.float32)
    (grad_keys, grad_values), grad_query = lax.scan(
        one_block, (zeros_kv, zeros_kv), jnp.arange(block_count, dtype=jnp.int32)
    )
    return (grad_query.reshape(keys.shape), grad_keys, grad_values)


def forward_pass(latent_rows, weights, groups, masks, block_rows, factor):
    qkv_rows, out_rows, up_rows, down_rows, gains, offsets = weights
    gains_full = gains.astype(jnp.float32)
    offsets_full = offsets.astype(jnp.float32)
    seq_count = groups.shape[0]
    seq_len = groups.shape[1]
    inputs_a = spread_rows(
        norm_rows(latent_rows, gains_full[0], offsets_full[0]).astype(jnp.bfloat16)
    )
    projected = jnp.einsum(
        "rd,tde->tre", inputs_a, qkv_rows, preferred_element_type=jnp.float32
    ).astype(jnp.bfloat16)
    local_heads = projected.shape[2] // HEAD_DIM
    shaped = projected.reshape(3, seq_count, seq_len, local_heads, HEAD_DIM)
    mixture, log_totals = lax.map(
        lambda element: attend_forward(
            element[0], element[1], element[2], element[3], element[4], block_rows, factor
        ),
        (shaped[0], shaped[1], shaped[2], groups, masks),
    )
    attended = mixture.reshape(seq_count * seq_len, local_heads * HEAD_DIM).astype(jnp.bfloat16)
    resid = latent_rows + settle_rows(
        jnp.einsum("rk,dk->rd", attended, out_rows, preferred_element_type=jnp.float32)
    )
    inputs_c = spread_rows(norm_rows(resid, gains_full[1], offsets_full[1]).astype(jnp.bfloat16))
    upward = jnp.dot(inputs_c, up_rows, preferred_element_type=jnp.float32)
    hidden = jax.nn.gelu(upward).astype(jnp.bfloat16)
    output = resid + settle_rows(
        jnp.einsum("rf,df->rd", hidden, down_rows, preferred_element_type=jnp.float32)
    )
    saved = (inputs_a, shaped, log_totals, attended, resid, inputs_c, upward, hidden)
    return (output, saved)


def backward_pass(latent_rows, grad_rows, weights, saved, groups, masks, block_rows, factor):
    qkv_rows, out_rows, up_rows, down_rows, gains, offsets = weights
    gains_full = gains.astype(jnp.float32)
    offsets_full = offsets.astype(jnp.float32)
    inputs_a, shaped, log_totals, attended, resid, inputs_c, upward, hidden = saved
    seq_count = groups.shape[0]
    seq_len = groups.shape[1]
    local_heads = shaped.shape[3]
    grad_z = spread_rows(grad_rows.astype(jnp.bfloat16))
    grad_down = jnp.einsum("rd,rf->df", grad_z, hidden, preferred_element_type=jnp.float32)
    grad_hidden = jnp.einsum("rd,df->rf", grad_z, down_rows, preferred_element_type=jnp.float32)
    gelu_pull = jax.vjp(jax.nn.gelu, upward)[1]
    grad_upward = gelu_pull(grad_hidden)[0].astype(jnp.bfloat16)
    grad_up = jnp.einsum("rd,rf->df", inputs_c, grad_upward, preferred_element_type=jnp.float32)
    grad_norm_two = settle_rows(
        jnp.einsum("rf,df->rd", grad_upward, up_rows, preferred_element_type=jnp.float32)
    )
    norm_pull_two = jax.vjp(norm_rows, resid, gains_full[1], offsets_full[1])[1]
    resid_part, gain_two, offset_two = norm_pull_two(grad_norm_two)
    grad_resid = grad_rows + resid_part
    grad_branch = spread_rows(grad_resid.astype(jnp.bfloat16))
    grad_out = jnp.einsum("rd,rk->dk", grad_branch, attended, preferred_element_type=jnp.float32)
    grad_attended = jnp.einsum(
        "rd,dk->rk", grad_branch, out_rows, preferred_element_type=jnp.float32
    )
    grad_attended = grad_attended.astype(jnp.bfloat16).reshape(
        seq_count, seq_len, local_heads, HEAD_DIM
    )
    grad_queries, grad_keys, grad_values = lax.map(
        lambda element: attend_backward(
            element[0],
            element[1],
            element[2],
            element[3],
            element[4],
            element[5],
            element[6],
            block_rows,
            factor,
        ),
        (shaped[0], shaped[1], shaped[2], grad_attended, log_totals, groups, masks),
    )
    grad_projected = (
        jnp.stack([grad_queries, grad_keys, grad_values])
        .reshape(3, seq_count * seq_len, local_heads * HEAD_DIM)
        .astype(jnp.bfloat16)
    )
    grad_qkv = jnp.einsum(
        "rd,tre->tde", inputs_a, grad_projected, preferred_element_type=jnp.float32
    )
    grad_norm_one = settle_rows(
        jnp.einsum("tre,tde->rd", grad_projected, qkv_rows, preferred_element_type=jnp.float32)
    )
    norm_pull_one = jax.vjp(norm_rows, latent_rows, gains_full[0], offsets_full[0])[1]
    rows_part, gain_one, offset_one = norm_pull_one(grad_norm_one)
    grad_latents = grad_resid + rows_part
    grad_gains = jnp.stack([gain_one, gain_two])
    grad_offsets = jnp.stack([offset_one, offset_two])
    return (grad_latents, (grad_qkv, grad_out, grad_up, grad_down, grad_gains, grad_offsets))


def add_trees(first_tree, second_tree):
    if first_tree is None:
        return second_tree
    return tuple((left + right for left, right in zip(first_tree, second_tree)))


def body(latents, group_ids, pad_mask, w_qkv, w_out, w_up, w_down, norm_gain, norm_bias, out_grad):
    micro_count = latents.shape[0]
    seq_len = group_ids.shape[2]
    block_rows = min(512, seq_len)
    factor = HEAD_DIM ** (-0.5)
    outputs = []
    input_grads = []
    totals = None
    for batch_index in range(micro_count):
        latent_rows = latents[batch_index]
        groups = group_ids[batch_index]
        masks = pad_mask[batch_index]
        forward_weights = (
            lax.all_gather(w_qkv, "dp", axis=1, tiled=True),
            lax.all_gather(w_out, "dp", axis=0, tiled=True),
            lax.all_gather(w_up, "dp", axis=0, tiled=True),
            lax.all_gather(w_down, "dp", axis=0, tiled=True),
            lax.all_gather(norm_gain, "dp", axis=1, tiled=True),
            lax.all_gather(norm_bias, "dp", axis=1, tiled=True),
        )
        output, saved = forward_pass(
            latent_rows, forward_weights, groups, masks, block_rows, factor
        )
        outputs.append(output)
        backward_weights = (
            lax.all_gather(w_qkv, "dp", axis=1, tiled=True),
            lax.all_gather(w_out, "dp", axis=0, tiled=True),
            lax.all_gather(w_up, "dp", axis=0, tiled=True),
            lax.all_gather(w_down, "dp", axis=0, tiled=True),
            lax.all_gather(norm_gain, "dp", axis=1, tiled=True),
            lax.all_gather(norm_bias, "dp", axis=1, tiled=True),
        )
        grad_latents, partials = backward_pass(
            latent_rows,
            out_grad[batch_index],
            backward_weights,
            saved,
            groups,
            masks,
            block_rows,
            factor,
        )
        input_grads.append(grad_latents)
        norm_sums = lax.psum((partials[4], partials[5]), "mp")
        shares = (
            lax.psum_scatter(partials[0], "dp", scatter_dimension=1, tiled=True),
            lax.psum_scatter(partials[1], "dp", scatter_dimension=0, tiled=True),
            lax.psum_scatter(partials[2], "dp", scatter_dimension=0, tiled=True),
            lax.psum_scatter(partials[3], "dp", scatter_dimension=0, tiled=True),
            lax.psum_scatter(norm_sums[0], "dp", scatter_dimension=1, tiled=True),
            lax.psum_scatter(norm_sums[1], "dp", scatter_dimension=1, tiled=True),
        )
        totals = add_trees(totals, shares)
    return (
        jnp.stack(outputs),
        jnp.stack(input_grads),
        totals[0],
        totals[1],
        totals[2],
        totals[3],
        totals[4],
        totals[5],
    )


def solution(mesh):
    return jax.shard_map(
        body,
        mesh=mesh,
        in_specs=(
            P(None, ("dp", "mp"), None),
            P(None, "dp", None),
            P(None, "dp", None),
            P(None, "dp", "mp"),
            P("dp", "mp"),
            P("dp", "mp"),
            P("dp", "mp"),
            P(None, "dp"),
            P(None, "dp"),
            P(None, ("dp", "mp"), None),
        ),
        out_specs=(
            P(None, ("dp", "mp"), None),
            P(None, ("dp", "mp"), None),
            P(None, "dp", "mp"),
            P("dp", "mp"),
            P("dp", "mp"),
            P("dp", "mp"),
            P(None, "dp"),
            P(None, "dp"),
        ),
        check_vma=False,
    )
```

profile of v0, /device:TPU:0, one launch (start us, length us, event | category | flops | bytes accessed | tf_op | source)
XLA Modules:
  0.0 1899.2 jit_solution(16451634394889164312)
XLA Ops:
  44.2 43.0 %all-gather.16.cloned.1.call-done = bf16[1024,1024]{1,0:T(8,128)(2,1)} async-done(((bf16[256,1024]{1,0:T(8,128)(2,1)}), bf16[1024,1024]{1,0:T(8,128)(2,1)}) %all-gather.16.cloned.1.call-update) | async-done | bytes 2097168 | tf_op jit(solution)/shard_map/all_gather | solution.py:18
  207.2 51.2 %reduce-scatter.23.cloned.1.call-done = f32[256,1024]{1,0:T(8,128)} async-done(((f32[1024,1024]{1,0:T(8,128)}), f32[256,1024]{1,0:T(8,128)}) %reduce-scatter.23.cloned.1.call-update) | async-done | bytes 1048592 | tf_op jit(solution)/shard_map/reduce_scatter | solution.py:22
  258.4 79.6 %reduce-scatter.27.cloned.1.call-done = f32[256,1024]{1,0:T(8,128)} async-done(((f32[1024,1024]{1,0:T(8,128)}), f32[256,1024]{1,0:T(8,128)}) %reduce-scatter.27.cloned.1.call-update) | async-done | bytes 1048592 | tf_op jit(solution)/shard_map/reduce_scatter | solution.py:22
  338.0 79.6 %reduce-scatter.31.cloned.1.call-done = f32[256,1024]{1,0:T(8,128)} async-done(((f32[1024,1024]{1,0:T(8,128)}), f32[256,1024]{1,0:T(8,128)}) %reduce-scatter.31.cloned.1.call-update) | async-done | bytes 1048592 | tf_op jit(solution)/shard_map/reduce_scatter | solution.py:22
  425.2 41.1 %all-gather.38.cloned.1.call-done = bf16[1024,1024]{1,0:T(8,128)(2,1)} async-done(((bf16[256,1024]{1,0:T(8,128)(2,1)}), bf16[1024,1024]{1,0:T(8,128)(2,1)}) %all-gather.38.cloned.1.call-update) | async-done | bytes 2097168 | tf_op jit(solution)/shard_map/all_gather | solution.py:18
  524.8 47.6 %all-gather.28.cloned.1.call-done = bf16[1024,1024]{1,0:T(8,128)(2,1)} async-done(((bf16[256,1024]{1,0:T(8,128)(2,1)}), bf16[1024,1024]{1,0:T(8,128)(2,1)}) %all-gather.28.cloned.1.call-update) | async-done | bytes 2097168 | tf_op jit(solution)/shard_map/all_gather | solution.py:18
  588.7 30.5 %all-gather.34.cloned.1.call-done = bf16[1024,1024]{1,0:T(8,128)(2,1)} async-done(((bf16[256,1024]{1,0:T(8,128)(2,1)}), bf16[1024,1024]{1,0:T(8,128)(2,1)}) %all-gather.34.cloned.1.call-update) | async-done | bytes 2097168 | tf_op jit(solution)/shard_map/all_gather | solution.py:18
  625.1 41.0 %all-gather.20.cloned.1.call-done = bf16[1024,1024]{1,0:T(8,128)(2,1)} async-done(((bf16[256,1024]{1,0:T(8,128)(2,1)}), bf16[1024,1024]{1,0:T(8,128)(2,1)}) %all-gather.20.cloned.1.call-update) | async-done | bytes 2097168 | tf_op jit(solution)/shard_map/all_gather | solution.py:18
  718.1 40.3 %all-gather.32.cloned.1.call-done = bf16[1024,1024]{1,0:T(8,128)(2,1)} async-done(((bf16[256,1024]{1,0:T(8,128)(2,1)}), bf16[1024,1024]{1,0:T(8,128)(2,1)}) %all-gather.32.cloned.1.call-update) | async-done | bytes 2097168 | tf_op jit(solution)/shard_map/all_gather | solution.py:18
  788.4 47.8 %reduce-scatter.39.cloned.1.call-done = f32[256,1024]{1,0:T(8,128)} async-done(((f32[1024,1024]{1,0:T(8,128)}), f32[256,1024]{1,0:T(8,128)}) %reduce-scatter.39.cloned.1.call-update) | async-done | bytes 1048592 | tf_op jit(solution)/shard_map/reduce_scatter | solution.py:22
  836.2 79.4 %reduce-scatter.35.cloned.1.call-done = f32[256,1024]{1,0:T(8,128)} async-done(((f32[1024,1024]{1,0:T(8,128)}), f32[256,1024]{1,0:T(8,128)}) %reduce-scatter.35.cloned.1.call-update) | async-done | bytes 1048592 | tf_op jit(solution)/shard_map/reduce_scatter | solution.py:22
  918.6 76.6 %reduce-scatter.29.cloned.1.call-done = f32[256,1024]{1,0:T(8,128)} async-done(((f32[1024,1024]{1,0:T(8,128)}), f32[256,1024]{1,0:T(8,128)}) %reduce-scatter.29.cloned.1.call-update) | async-done | bytes 1048592 | tf_op jit(solution)/shard_map/reduce_scatter | solution.py:22
  995.2 79.6 %reduce-scatter.43.cloned.1.call-done = f32[256,1024]{1,0:T(8,128)} async-done(((f32[1024,1024]{1,0:T(8,128)}), f32[256,1024]{1,0:T(8,128)}) %reduce-scatter.43.cloned.1.call-update) | async-done | bytes 1048592 | tf_op jit(solution)/shard_map/reduce_scatter | solution.py:22
  1074.8 79.5 %reduce-scatter.25.cloned.1.call-done = f32[256,1024]{1,0:T(8,128)} async-done(((f32[1024,1024]{1,0:T(8,128)}), f32[256,1024]{1,0:T(8,128)}) %reduce-scatter.25.cloned.1.call-update) | async-done | bytes 1048592 | tf_op jit(solution)/shard_map/reduce_scatter | solution.py:22
  1159.3 74.6 %reduce-scatter.33.cloned.1.call-done = f32[256,1024]{1,0:T(8,128)} async-done(((f32[1024,1024]{1,0:T(8,128)}), f32[256,1024]{1,0:T(8,128)}) %reduce-scatter.33.cloned.1.call-update) | async-done | bytes 1048592 | tf_op jit(solution)/shard_map/reduce_scatter | solution.py:22
  1240.6 45.2 %all-gather.36.cloned.1.call-done = bf16[1024,1024]{1,0:T(8,128)(2,1)} async-done(((bf16[256,1024]{1,0:T(8,128)(2,1)}), bf16[1024,1024]{1,0:T(8,128)(2,1)}) %all-gather.36.cloned.1.call-update) | async-done | bytes 2097168 | tf_op jit(solution)/shard_map/all_gather | solution.py:18
  1457.1 79.5 %reduce-scatter.45.cloned.1.call-done = f32[256,1024]{1,0:T(8,128)} async-done(((f32[1024,1024]{1,0:T(8,128)}), f32[256,1024]{1,0:T(8,128)}) %reduce-scatter.45.cloned.1.call-update) | async-done | bytes 1048592 | tf_op jit(solution)/shard_map/reduce_scatter | solution.py:22
  1536.6 79.5 %reduce-scatter.41.cloned.1.call-done = f32[256,1024]{1,0:T(8,128)} async-done(((f32[1024,1024]{1,0:T(8,128)}), f32[256,1024]{1,0:T(8,128)}) %reduce-scatter.41.cloned.1.call-update) | async-done | bytes 1048592 | tf_op jit(solution)/shard_map/reduce_scatter | solution.py:22
  1631.0 40.3 %reduce-scatter.53.cloned.1.call-done = f32[128,1024]{0,1:T(8,128)} async-done(((f32[1024,1024]{0,1:T(8,128)}), f32[128,1024]{0,1:T(8,128)}) %reduce-scatter.53.cloned.1.call-update) | async-done | bytes 524304 | tf_op jit(solution)/shard_map/reduce_scatter | solution.py:260
  1682.7 39.2 %reduce-scatter.47.cloned.1.call-done = f32[3,128,256]{1,2,0:T(8,128)} async-done(((f32[3,1024,256]{1,2,0:T(8,128)}), f32[3,128,256]{1,2,0:T(8,128)}) %reduce-scatter.47.cloned.1.call-update) | async-done | bytes 393232 | tf_op jit(solution)/shard_map/reduce_scatter | solution.py:257
  1730.3 28.7 %reduce-scatter.55.cloned.1.call-done = f32[128,2]{1,0:T(8,128)} async-done(((f32[1024,2]{1,0:T(8,128)}), f32[128,2]{1,0:T(8,128)}) %reduce-scatter.55.cloned.1.call-update) | async-done | bytes 1040
  1759.9 36.7 %reduce-scatter.57.cloned.1.call-done = f32[128,2]{1,0:T(8,128)} async-done(((f32[1024,2]{1,0:T(8,128)}), f32[128,2]{1,0:T(8,128)}) %reduce-scatter.57.cloned.1.call-update) | async-done | bytes 1040
  1809.7 42.1 %reduce-scatter.51.cloned.1.call-done = f32[128,1024]{1,0:T(8,128)} async-done(((f32[1024,1024]{1,0:T(8,128)}), f32[128,1024]{1,0:T(8,128)}) %reduce-scatter.51.cloned.1.call-update) | async-done | bytes 524304 | tf_op jit(solution)/shard_map/reduce_scatter | solution.py:259
  1851.8 40.0 %reduce-scatter.49.cloned.1.call-done = f32[128,256]{1,0:T(8,128)} async-done(((f32[1024,256]{1,0:T(8,128)}), f32[128,256]{1,0:T(8,128)}) %reduce-scatter.49.cloned.1.call-update) | async-done | bytes 131088 | tf_op jit(solution)/shard_map/reduce_scatter | solution.py:258
  (673 shorter events, 643.3 us)
Async XLA Ops:
  35.1 223.3 %reduce-scatter.23.cloned.1.call-start = ((), (), s32[]{:S(2)}) async-start(), calls=%async_computation.20 | async-start | bytes 5242880 | tf_op jit(solution)/shard_map/reduce_scatter | solution.py:22
  108.6 229.4 %reduce-scatter.27.cloned.1.call-start = ((), (), s32[]{:S(2)}) async-start(), calls=%async_computation.26 | async-start | bytes 5242880 | tf_op jit(solution)/shard_map/reduce_scatter | solution.py:22
  155.4 262.1 %reduce-scatter.31.cloned.1.call-start = ((), (), s32[]{:S(2)}) async-start(), calls=%async_computation.30 | async-start | bytes 5242880 | tf_op jit(solution)/shard_map/reduce_scatter | solution.py:22
  202.5 263.8 %all-gather.38.cloned.1.call-start = ((), (), s32[]{:S(2)}) async-start(), calls=%async_computation.37 | async-start | bytes 2621440 | tf_op jit(solution)/shard_map/all_gather | solution.py:18
  205.8 289.2 %all-gather.24.cloned.1.call-start = ((), (), s32[]{:S(2)}) async-start(), calls=%async_computation.23 | async-start | bytes 2359296 | tf_op jit(solution)/shard_map/all_gather | solution.py:228
  206.5 318.3 %all-gather.22.cloned.1.call-start = ((), (), s32[]{:S(2)}) async-start(), calls=%async_computation.22 | async-start | bytes 2359296 | tf_op jit(solution)/shard_map/all_gather | solution.py:227
  207.1 365.3 %all-gather.28.cloned.1.call-start = ((), (), s32[]{:S(2)}) async-start(), calls=%async_computation.27 | async-start | bytes 2621440 | tf_op jit(solution)/shard_map/all_gather | solution.py:18
  423.0 243.0 %all-gather.20.cloned.1.call-start = ((), (), s32[]{:S(2)}) async-start(), calls=%async_computation.21 | async-start | bytes 2621440 | tf_op jit(solution)/shard_map/all_gather | solution.py:18
  423.8 288.5 %all-gather.42.cloned.1.call-start = ((), (), s32[]{:S(2)}) async-start(), calls=%async_computation.41 | async-start | bytes 2621440 | tf_op jit(solution)/shard_map/all_gather | solution.py:18
  424.4 334.1 %all-gather.32.cloned.1.call-start = ((), (), s32[]{:S(2)}) async-start(), calls=%async_computation.31 | async-start | bytes 2621440 | tf_op jit(solution)/shard_map/all_gather | solution.py:18
  424.9 411.3 %reduce-scatter.39.cloned.1.call-start = ((), (), s32[]{:S(2)}) async-start(), calls=%async_computation.38 | async-start | bytes 5242880 | tf_op jit(solution)/shard_map/reduce_scatter | solution.py:22
  588.2 327.4 %reduce-scatter.35.cloned.1.call-start = ((), (), s32[]{:S(2)}) async-start(), calls=%async_computation.34 | async-start | bytes 5242880 | tf_op jit(solution)/shard_map/reduce_scatter | solution.py:22
  681.8 313.4 %reduce-scatter.29.cloned.1.call-start = ((), (), s32[]{:S(2)}) async-start(), calls=%async_computation.28 | async-start | bytes 5242880 | tf_op jit(solution)/shard_map/reduce_scatter | solution.py:22
  688.8 385.9 %reduce-scatter.43.cloned.1.call-start = ((), (), s32[]{:S(2)}) async-start(), calls=%async_computation.42 | async-start | bytes 5242880 | tf_op jit(solution)/shard_map/reduce_scatter | solution.py:22
  774.2 380.1 %reduce-scatter.25.cloned.1.call-start = ((), (), s32[]{:S(2)}) async-start(), calls=%async_computation.24 | async-start | bytes 5242880 | tf_op jit(solution)/shard_map/reduce_scatter | solution.py:22
  781.2 452.7 %reduce-scatter.33.cloned.1.call-start = ((), (), s32[]{:S(2)}) async-start(), calls=%async_computation.32 | async-start | bytes 5242880 | tf_op jit(solution)/shard_map/reduce_scatter | solution.py:22
  788.1 497.7 %all-gather.36.cloned.1.call-start = ((), (), s32[]{:S(2)}) async-start(), calls=%async_computation.35 | async-start | bytes 2621440 | tf_op jit(solution)/shard_map/all_gather | solution.py:18
  1240.5 216.6 %reduce-scatter.37.cloned.1.call-start = ((), (), s32[]{:S(2)}) async-start(), calls=%async_computation.36 | async-start | bytes 5242880 | tf_op jit(solution)/shard_map/reduce_scatter | solution.py:22
  1368.6 247.5 %reduce-scatter.41.cloned.1.call-start = ((), (), s32[]{:S(2)}) async-start(), calls=%async_computation.40 | async-start | bytes 5242880 | tf_op jit(solution)/shard_map/reduce_scatter | solution.py:22
  1413.7 257.6 %reduce-scatter.53.cloned.1.call-start = ((), (), s32[]{:S(2)}) async-start(), calls=%async_computation.48 | async-start | bytes 4718592 | tf_op jit(solution)/shard_map/reduce_scatter | solution.py:260
  1428.1 293.8 %reduce-scatter.47.cloned.1.call-start = ((), (), s32[]{:S(2)}) async-start(), calls=%async_computation.45 | async-start | bytes 3538944 | tf_op jit(solution)/shard_map/reduce_scatter | solution.py:257
  1437.9 321.1 %reduce-scatter.55.cloned.1.call-start = ((), (), s32[]{:S(2)}) async-start(), calls=%async_computation.49 | async-start | bytes 589824
  1621.1 230.8 %reduce-scatter.51.cloned.1.call-start = ((), (), s32[]{:S(2)}) async-start(), calls=%async_computation.47 | async-start | bytes 4718592 | tf_op jit(solution)/shard_map/reduce_scatter | solution.py:259
  1631.0 260.8 %reduce-scatter.49.cloned.1.call-start = ((), (), s32[]{:S(2)}) async-start(), calls=%async_computation.46 | async-start | bytes 1179648 | tf_op jit(solution)/shard_map/reduce_scatter | solution.py:258
  (168 other events, 6482.1 us)
Sparse Core Ops, SparseCore 0:
  41.2 45.9 all-gather.15
  136.0 44.9 all-gather.29
  183.1 75.2 reduce-scatter.22
  260.7 77.2 reduce-scatter.26
  340.3 77.2 reduce-scatter.30
  419.8 46.4 all-gather.37
  526.4 45.9 all-gather.27
  574.5 44.6 all-gather.33
  667.6 44.6 all-gather.41
  713.8 44.6 all-gather.31
  760.7 75.4 reduce-scatter.38
  838.3 77.2 reduce-scatter.34
  917.9 77.2 reduce-scatter.28
  997.5 77.2 reduce-scatter.42
  1077.0 77.2 reduce-scatter.24
  1156.6 77.2 reduce-scatter.32
  1239.3 46.4 all-gather.35
  1334.2 44.9 all-gather.39
  1381.6 75.4 reduce-scatter.36
  1459.2 77.2 reduce-scatter.44
  1538.8 77.2 reduce-scatter.40
  1619.4 51.8 reduce-scatter.52
  1675.6 46.2 reduce-scatter.46
  1800.5 51.3 reduce-scatter.50
  (9 shorter events, 320.8 us)
where the time goes:
time: 1910 us; the launch traced here: 1900 us
  waiting for transfers between devices  1480 us (77%)
  matrix products  225 us (12%)
  other arithmetic  57.3 us (3%)
  local copies, waits for them, and re-layouts  50.2 us (3%)
  blocking collectives  40.2 us (2%)
  loops' own time  20.7 us (1%)
    reduce_scatter x12, waiting for transfers between devices, settle_rows(): return lax.psum_scatter(partial_rows, 'mp', scatter_dimension=0, tiled=True)  815 us
    all_gather x12, waiting for transfers between devices, spread_rows(): return lax.all_gather(rows_local, 'mp', axis=0, tiled=True)  384 us
    unnamed x35, waiting for transfers between devices  71.6 us
    reduce_scatter x1, waiting for transfers between devices, body(): lax.psum_scatter(partials[2], 'dp', scatter_dimension=0, tiled=True)  42.1 us
    reduce_scatter x1, waiting for transfers between devices, body(): lax.psum_scatter(partials[3], 'dp', scatter_dimension=0, tiled=True)  40.3 us
    reduce_scatter x1, waiting for transfers between devices, body(): lax.psum_scatter(partials[1], 'dp', scatter_dimension=0, tiled=True)  40 us
    reduce_scatter x1, waiting for transfers between devices, body(): lax.psum_scatter(partials[0], 'dp', scatter_dimension=1, tiled=True)  39.2 us
  transfers between devices with their start and end apart: 33, of which 32 were waited for; matrix products, arithmetic and copies ran while one was open for 17% of the time, Pallas kernels for 0%

commit v1 on v0

--- a/solution.py
+++ b/solution.py
@@ -5,6 +5,17 @@
 
 HEAD_DIM = 128
 epsilon = 1e-05
+
+
+def collect(x, axis, dim):
+    ways = lax.axis_size(axis)
+    pieces = [x]
+    for far in range(1, ways):
+        pieces.append(
+            lax.ppermute(pieces[far - 1], axis, [(d, (d - 1) % ways) for d in range(ways)])
+        )
+    line = jnp.concatenate(pieces, axis=dim)
+    return jnp.roll(line, lax.axis_index(axis) * x.shape[dim], axis=dim)
 
 
 def norm_rows(values, scaling, offset):
@@ -15,7 +26,7 @@
 
 
 def spread_rows(rows_local):
-    return lax.all_gather(rows_local, "mp", axis=0, tiled=True)
+    return collect(rows_local, "mp", 0)
 
 
 def settle_rows(partial_rows):

time: 1910 us -> 1840 us (0.963)
  waiting for transfers between devices: 1480 us -> 1240 us
  other arithmetic: 57.3 us -> 180 us
  starting transfers between devices: 4.37 us -> 77.4 us
  matrix products: 225 us -> 198 us
    ppermute x0 -> x36, waiting for transfers between devices: none -> 576 us  [collect(): lax.ppermute(pieces[far - 1], axis, [(d, (d - 1) % ways) for d in range(w...]
    all_gather x12 -> x0, waiting for transfers between devices: 384 us -> none  [spread_rows(): return lax.all_gather(rows_local, 'mp', axis=0, tiled=True)]
    reduce_scatter x12, waiting for transfers between devices: 815 us -> 446 us  [settle_rows(): return lax.psum_scatter(partial_rows, 'mp', scatter_dimension=0, tiled=True)]
    concatenate x0 -> x9, other arithmetic: none -> 90.3 us  [collect(): return jnp.roll(line, lax.axis_index(axis) * x.shape[dim], axis=dim)]
    ppermute x0 -> x36, starting transfers between devices: none -> 75.8 us  [collect(): lax.ppermute(pieces[far - 1], axis, [(d, (d - 1) % ways) for d in range(w...]
    dynamic_slice x0 -> x3, other arithmetic: none -> 34 us  [collect(): return jnp.roll(line, lax.axis_index(axis) * x.shape[dim], axis=dim)]
    all_gather x1, waiting for transfers between devices: 28.7 us -> 0.01 us  [body(): lax.all_gather(w_down, 'dp', axis=0, tiled=True)]
    reduce_scatter x1, waiting for transfers between devices: 39.2 us -> 13.3 us  [body(): lax.psum_scatter(partials[0], 'dp', scatter_dimension=1, tiled=True)]
  transfers between devices with their start and end apart: 33 -> 57, of which waited for: 32 -> 44; matrix products, arithmetic and copies ran while one was open for 17% -> 21% of each run, Pallas kernels for 0% -> 0%
where the time goes in v1:
time: 1840 us; the launch traced here: 1830 us
  waiting for transfers between devices  1240 us (67%)
  matrix products  198 us (11%)
  other arithmetic  180 us (10%)
  starting transfers between devices  77.4 us (4%)
  local copies, waits for them, and re-layouts  60.7 us (3%)
  blocking collectives  40 us (2%)
  loops' own time  20.6 us (1%)
    ppermute x36, waiting for transfers between devices, collect(): lax.ppermute(pieces[far - 1], axis, [(d, (d - 1) % ways) for d in range(w...  576 us
    reduce_scatter x12, waiting for transfers between devices, settle_rows(): return lax.psum_scatter(partial_rows, 'mp', scatter_dimension=0, tiled=True)  446 us
    concatenate x9, other arithmetic, collect(): return jnp.roll(line, lax.axis_index(axis) * x.shape[dim], axis=dim)  90.3 us
    ppermute x36, starting transfers between devices, collect(): lax.ppermute(pieces[far - 1], axis, [(d, (d - 1) % ways) for d in range(w...  75.8 us
    unnamed x23, waiting for transfers between devices  66 us
    reduce_scatter x1, waiting for transfers between devices, body(): lax.psum_scatter(partials[2], 'dp', scatter_dimension=0, tiled=True)  55.1 us
    reduce_scatter x1, waiting for transfers between devices, body(): lax.psum_scatter(partials[3], 'dp', scatter_dimension=0, tiled=True)  42.6 us
    reduce_scatter x1, waiting for transfers between devices, body(): lax.psum_scatter(partials[1], 'dp', scatter_dimension=0, tiled=True)  40.1 us
  transfers between devices with their start and end apart: 57, of which 44 were waited for; matrix products, arithmetic and copies ran while one was open for 21% of the time, Pallas kernels for 0%

profile of v1, /device:TPU:0, one launch (start us, length us, event | category | flops | bytes accessed | tf_op | source)
XLA Modules:
  0.0 1833.1 jit_solution(7048826990136755538)
XLA Ops:
  142.9 31.8 %collective-permute-done.7 = bf16[256,1024]{1,0:T(8,128)(2,1)S(1)} collective-permute-done((bf16[256,1024]{1,0:T(8,128)(2,1)S(1)}, bf16[256,1024]{1,0:T(8,128)(2,1)S(1)}, u32[]{:S(2)}, u32[]{:S(2)}) %collective-permute-start.7) | collective-permute-done | bytes 524320 | tf_op jit(solution)/shard_map/ppermute | solution.py:15
  174.7 40.8 %collective-permute-done.8 = bf16[256,1024]{1,0:T(8,128)(2,1)S(1)} collective-permute-done((bf16[256,1024]{1,0:T(8,128)(2,1)S(1)}, bf16[256,1024]{1,0:T(8,128)(2,1)S(1)}, u32[]{:S(2)}, u32[]{:S(2)}) %collective-permute-start.8) | collective-permute-done | bytes 524320 | tf_op jit(solution)/shard_map/ppermute | solution.py:15
  247.0 35.7 %collective-permute-done.12 = bf16[256,1024]{1,0:T(8,128)(2,1)S(1)} collective-permute-done((bf16[256,1024]{1,0:T(8,128)(2,1)S(1)}, bf16[256,1024]{1,0:T(8,128)(2,1)S(1)}, u32[]{:S(2)}, u32[]{:S(2)}) %collective-permute-start.12) | collective-permute-done | bytes 524320 | tf_op jit(solution)/shard_map/ppermute | solution.py:15
  282.7 36.1 %collective-permute-done.13 = bf16[256,1024]{1,0:T(8,128)(2,1)S(1)} collective-permute-done((bf16[256,1024]{1,0:T(8,128)(2,1)S(1)}, bf16[256,1024]{1,0:T(8,128)(2,1)S(1)}, u32[]{:S(2)}, u32[]{:S(2)}) %collective-permute-start.13) | collective-permute-done | bytes 524320 | tf_op jit(solution)/shard_map/ppermute | solution.py:15
  318.8 25.8 %collective-permute-done.14 = bf16[256,1024]{1,0:T(8,128)(2,1)S(1)} collective-permute-done((bf16[256,1024]{1,0:T(8,128)(2,1)S(1)}, bf16[256,1024]{1,0:T(8,128)(2,1)S(1)}, u32[]{:S(2)}, u32[]{:S(2)}) %collective-permute-start.14) | collective-permute-done | bytes 524320 | tf_op jit(solution)/shard_map/ppermute | solution.py:15
  381.4 73.5 %reduce-scatter.31.cloned.1.call-done = f32[256,1024]{1,0:T(8,128)} async-done(((f32[1024,1024]{1,0:T(8,128)}), f32[256,1024]{1,0:T(8,128)}) %reduce-scatter.31.cloned.1.call-update) | async-done | bytes 1048592 | tf_op jit(solution)/shard_map/reduce_scatter | solution.py:33
  556.7 22.9 %collective-permute-done.18 = bf16[256,1024]{1,0:T(8,128)(2,1)S(1)} collective-permute-done((bf16[256,1024]{1,0:T(8,128)(2,1)S(1)}, bf16[256,1024]{1,0:T(8,128)(2,1)S(1)}, u32[]{:S(2)}, u32[]{:S(2)}) %collective-permute-start.18) | collective-permute-done | bytes 524320 | tf_op jit(solution)/shard_map/ppermute | solution.py:15
  584.0 23.3 %collective-permute-done.3 = bf16[256,1024]{1,0:T(8,128)(2,1)S(1)} collective-permute-done((bf16[256,1024]{1,0:T(8,128)(2,1)S(1)}, bf16[256,1024]{1,0:T(8,128)(2,1)S(1)}, u32[]{:S(2)}, u32[]{:S(2)}) %collective-permute-start.3) | collective-permute-done | bytes 524320 | tf_op jit(solution)/shard_map/ppermute | solution.py:15
  607.3 30.9 %collective-permute-done.19 = bf16[256,1024]{1,0:T(8,128)(2,1)S(1)} collective-permute-done((bf16[256,1024]{1,0:T(8,128)(2,1)S(1)}, bf16[256,1024]{1,0:T(8,128)(2,1)S(1)}, u32[]{:S(2)}, u32[]{:S(2)}) %collective-permute-start.19) | collective-permute-done | bytes 524320 | tf_op jit(solution)/shard_map/ppermute | solution.py:15
  733.9 30.1 %collective-permute-done.30 = bf16[256,1024]{1,0:T(8,128)(2,1)S(1)} collective-permute-done((bf16[256,1024]{1,0:T(8,128)(2,1)S(1)}, bf16[256,1024]{1,0:T(8,128)(2,1)S(1)}, u32[]{:S(2)}, u32[]{:S(2)}) %collective-permute-start.30) | collective-permute-done | bytes 524320 | tf_op jit(solution)/shard_map/ppermute | solution.py:15
  764.0 30.9 %collective-permute-done.15 = bf16[256,1024]{1,0:T(8,128)(2,1)S(1)} collective-permute-done((bf16[256,1024]{1,0:T(8,128)(2,1)S(1)}, bf16[256,1024]{1,0:T(8,128)(2,1)S(1)}, u32[]{:S(2)}, u32[]{:S(2)}) %collective-permute-start.15) | collective-permute-done | bytes 524320 | tf_op jit(solution)/shard_map/ppermute | solution.py:15
  794.9 22.9 %collective-permute-done.31 = bf16[256,1024]{1,0:T(8,128)(2,1)S(1)} collective-permute-done((bf16[256,1024]{1,0:T(8,128)(2,1)S(1)}, bf16[256,1024]{1,0:T(8,128)(2,1)S(1)}, u32[]{:S(2)}, u32[]{:S(2)}) %collective-permute-start.31) | collective-permute-done | bytes 524320 | tf_op jit(solution)/shard_map/ppermute | solution.py:15
  895.9 41.1 %reduce-scatter.29.cloned.1.call-done = f32[256,1024]{1,0:T(8,128)} async-done(((f32[1024,1024]{1,0:T(8,128)}), f32[256,1024]{1,0:T(8,128)}) %reduce-scatter.29.cloned.1.call-update) | async-done | bytes 1048592 | tf_op jit(solution)/shard_map/reduce_scatter | solution.py:33
  937.0 79.4 %reduce-scatter.25.cloned.1.call-done = f32[256,1024]{1,0:T(8,128)} async-done(((f32[1024,1024]{1,0:T(8,128)}), f32[256,1024]{1,0:T(8,128)}) %reduce-scatter.25.cloned.1.call-update) | async-done | bytes 1048592 | tf_op jit(solution)/shard_map/reduce_scatter | solution.py:33
  1016.5 79.7 %reduce-scatter.43.cloned.1.call-done = f32[256,1024]{1,0:T(8,128)} async-done(((f32[1024,1024]{1,0:T(8,128)}), f32[256,1024]{1,0:T(8,128)}) %reduce-scatter.43.cloned.1.call-update) | async-done | bytes 1048592 | tf_op jit(solution)/shard_map/reduce_scatter | solution.py:33
  1101.1 74.5 %reduce-scatter.33.cloned.1.call-done = f32[256,1024]{1,0:T(8,128)} async-done(((f32[1024,1024]{1,0:T(8,128)}), f32[256,1024]{1,0:T(8,128)}) %reduce-scatter.33.cloned.1.call-update) | async-done | bytes 1048592 | tf_op jit(solution)/shard_map/reduce_scatter | solution.py:33
  1306.1 23.5 %collective-permute-done.29 = bf16[256,1024]{1,0:T(8,128)(2,1)} collective-permute-done((bf16[256,1024]{1,0:T(8,128)(2,1)}, bf16[256,1024]{1,0:T(8,128)(2,1)}, u32[]{:S(2)}, u32[]{:S(2)}) %collective-permute-start.29) | collective-permute-done | bytes 524320 | tf_op jit(solution)/shard_map/ppermute | solution.py:15
  1397.9 22.6 %while.144 = (s32[]{:T(128)}, f32[1024,2,128]{0,2,1:T(8,128)S(1)}, f32[1024,2,128]{0,2,1:T(8,128)}, bf16[2,512,2,128]{3,1,2,0:T(8,128)(2,1)}, s32[2]{0:T(128)S(1...) while((s32[]{:T(128)}, f32[1024,2,128]{0,2,1:T(8,128)S(1)}, ...), condition=%wide.region_35.37_spmd.clone, body=%wide.region_33.36_spmd.clone.sunk | while | flops 1361445376 | bytes 55624116 | solution.py:116
  1470.6 79.5 %reduce-scatter.37.cloned.1.call-done = f32[256,1024]{1,0:T(8,128)} async-done(((f32[1024,1024]{1,0:T(8,128)}), f32[256,1024]{1,0:T(8,128)}) %reduce-scatter.37.cloned.1.call-update) | async-done | bytes 1048592 | tf_op jit(solution)/shard_map/reduce_scatter | solution.py:33
  1609.1 29.0 %reduce-scatter.55.cloned.1.call-done = f32[128,2]{1,0:T(8,128)} async-done(((f32[1024,2]{1,0:T(8,128)}), f32[128,2]{1,0:T(8,128)}) %reduce-scatter.55.cloned.1.call-update) | async-done | bytes 1040
  1639.0 36.1 %reduce-scatter.57.cloned.1.call-done = f32[128,2]{1,0:T(8,128)} async-done(((f32[1024,2]{1,0:T(8,128)}), f32[128,2]{1,0:T(8,128)}) %reduce-scatter.57.cloned.1.call-update) | async-done | bytes 1040
  1688.3 42.6 %reduce-scatter.53.cloned.1.call-done = f32[128,1024]{1,0:T(8,128)} async-done(((f32[1024,1024]{1,0:T(8,128)}), f32[128,1024]{1,0:T(8,128)}) %reduce-scatter.53.cloned.1.call-update) | async-done | bytes 524304 | tf_op jit(solution)/shard_map/reduce_scatter | solution.py:271
  1730.9 55.1 %reduce-scatter.51.cloned.1.call-done = f32[128,1024]{1,0:T(8,128)} async-done(((f32[1024,1024]{1,0:T(8,128)}), f32[128,1024]{1,0:T(8,128)}) %reduce-scatter.51.cloned.1.call-update) | async-done | bytes 524304 | tf_op jit(solution)/shard_map/reduce_scatter | solution.py:270
  1786.0 40.1 %reduce-scatter.49.cloned.1.call-done = f32[128,256]{1,0:T(8,128)} async-done(((f32[1024,256]{1,0:T(8,128)}), f32[128,256]{1,0:T(8,128)}) %reduce-scatter.49.cloned.1.call-update) | async-done | bytes 131088 | tf_op jit(solution)/shard_map/reduce_scatter | solution.py:269
  (770 shorter events, 891.8 us)
Async XLA Ops:
  7.2 81.6 %all-gather.4.cloned.1.call-start = ((), (), s32[]{:S(2)}) async-start(), calls=%async_computation.18 | async-start | bytes 1769472 | tf_op jit(solution)/shard_map/all_gather | solution.py:236
  9.2 372.2 %reduce-scatter.23.cloned.1.call-start = ((), (), s32[]{:S(2)}) async-start(), calls=%async_computation.19 | async-start | bytes 5242880 | tf_op jit(solution)/shard_map/reduce_scatter | solution.py:33
  113.3 268.1 %reduce-scatter.27.cloned.1.call-start = ((), (), s32[]{:S(2)}) async-start(), calls=%async_computation.23 | async-start | bytes 5242880 | tf_op jit(solution)/shard_map/reduce_scatter | solution.py:33
  246.8 208.1 %reduce-scatter.31.cloned.1.call-start = ((), (), s32[]{:S(2)}) async-start(), calls=%async_computation.25 | async-start | bytes 5242880 | tf_op jit(solution)/shard_map/reduce_scatter | solution.py:33
  376.5 154.3 %all-gather.6.cloned.1.call-start = ((), (), s32[]{:S(2)}) async-start(), calls=%async_computation.20 | async-start | bytes 2359296 | tf_op jit(solution)/shard_map/all_gather | solution.py:238
  377.1 160.4 %all-gather.8.cloned.1.call-start = ((), (), s32[]{:S(2)}) async-start(), calls=%async_computation.21 | async-start | bytes 2359296 | tf_op jit(solution)/shard_map/all_gather | solution.py:239
  381.3 79.9 %collective-permute-start.24 = (bf16[256,1024]{1,0:T(8,128)(2,1)}, bf16[256,1024]{1,0:T(8,128)(2,1)}, u32[]{:S(2)}, u32[]{:S(2)}) collective-permute-start(bf16[256,1024]{1,0:T(8,128)(2,1)} %get-tuple-element.1060), channel_id=1, source_target_pairs={{0,3},{1,0},{2,1},{3,2},{4,7},{5,4},{6,5},{7,6},{8,11},{9,8},{10,9... | collective-permute-start | bytes 1572872 | tf_op jit(solution)/shard_map/ppermute | solution.py:15
  381.3 510.2 %reduce-scatter.39.cloned.1.call-start = ((), (), s32[]{:S(2)}) async-start(), calls=%async_computation.29 | async-start | bytes 5242880 | tf_op jit(solution)/shard_map/reduce_scatter | solution.py:33
  551.4 340.2 %reduce-scatter.35.cloned.1.call-start = ((), (), s32[]{:S(2)}) async-start(), calls=%async_computation.27 | async-start | bytes 5242880 | tf_op jit(solution)/shard_map/reduce_scatter | solution.py:33
  714.4 222.6 %reduce-scatter.29.cloned.1.call-start = ((), (), s32[]{:S(2)}) async-start(), calls=%async_computation.24 | async-start | bytes 5242880 | tf_op jit(solution)/shard_map/reduce_scatter | solution.py:33
  721.3 295.1 %reduce-scatter.25.cloned.1.call-start = ((), (), s32[]{:S(2)}) async-start(), calls=%async_computation.22 | async-start | bytes 5242880 | tf_op jit(solution)/shard_map/reduce_scatter | solution.py:33
  728.6 367.6 %reduce-scatter.43.cloned.1.call-start = ((), (), s32[]{:S(2)}) async-start(), calls=%async_computation.31 | async-start | bytes 5242880 | tf_op jit(solution)/shard_map/reduce_scatter | solution.py:33
  733.8 61.0 %collective-permute-start.15 = (bf16[256,1024]{1,0:T(8,128)(2,1)S(1)}, bf16[256,1024]{1,0:T(8,128)(2,1)S(1)}, u32[]{:S(2)}, u32[]{:S(2)}) collective-permute-start(bf16[256,1024]{1,0:T(8,128)(2,1)S(1)} %get-tuple-element.1087), channel_id=1, source_target_pairs={{0,3},{1,0},{2,1},{3,2},{4,7},{5,4},{6,5},{7,6},{8,11},{9,8},{10,9... | collective-permute-start | bytes 1572872 | tf_op jit(solution)/shard_map/ppermute | solution.py:15
  884.6 291.0 %reduce-scatter.33.cloned.1.call-start = ((), (), s32[]{:S(2)}) async-start(), calls=%async_computation.26 | async-start | bytes 5242880 | tf_op jit(solution)/shard_map/reduce_scatter | solution.py:33
  891.4 560.6 %reduce-scatter.45.cloned.1.call-start = ((), (), s32[]{:S(2)}) async-start(), calls=%async_computation.32 | async-start | bytes 5242880 | tf_op jit(solution)/shard_map/reduce_scatter | solution.py:33
  1275.5 195.1 %reduce-scatter.41.cloned.1.call-start = ((), (), s32[]{:S(2)}) async-start(), calls=%async_computation.30 | async-start | bytes 5242880 | tf_op jit(solution)/shard_map/reduce_scatter | solution.py:33
  1301.7 69.5 %collective-permute-start.22 = (bf16[256,1024]{1,0:T(8,128)(2,1)}, bf16[256,1024]{1,0:T(8,128)(2,1)}, u32[]{:S(2)}, u32[]{:S(2)}) collective-permute-start(bf16[256,1024]{1,0:T(8,128)(2,1)} %collective-permute-done.21), channel_id=1, source_target_pairs={{0,3},{1,0},{2,1},{3,2},{4,7},{5,4},{6,5},{7,6},{8,11},{9,8},{10,9... | collective-permute-start | bytes 1572872 | tf_op jit(solution)/shard_map/ppermute | solution.py:15
  1371.2 179.0 %reduce-scatter.37.cloned.1.call-start = ((), (), s32[]{:S(2)}) async-start(), calls=%async_computation.28 | async-start | bytes 5242880 | tf_op jit(solution)/shard_map/reduce_scatter | solution.py:33
  1429.7 171.1 %reduce-scatter.47.cloned.1.call-start = ((), (), s32[]{:S(2)}) async-start(), calls=%async_computation.33 | async-start | bytes 3538944 | tf_op jit(solution)/shard_map/reduce_scatter | solution.py:268
  1440.4 197.8 %reduce-scatter.55.cloned.1.call-start = ((), (), s32[]{:S(2)}) async-start(), calls=%async_computation.37 | async-start | bytes 589824
  1554.0 121.2 %reduce-scatter.57.cloned.1.call-start = ((), (), s32[]{:S(2)}) async-start(), calls=%async_computation.38 | async-start | bytes 589824
  1555.2 175.7 %reduce-scatter.53.cloned.1.call-start = ((), (), s32[]{:S(2)}) async-start(), calls=%async_computation.36 | async-start | bytes 4718592 | tf_op jit(solution)/shard_map/reduce_scatter | solution.py:271
  1565.9 220.1 %reduce-scatter.51.cloned.1.call-start = ((), (), s32[]{:S(2)}) async-start(), calls=%async_computation.35 | async-start | bytes 4718592 | tf_op jit(solution)/shard_map/reduce_scatter | solution.py:270
  1577.9 248.2 %reduce-scatter.49.cloned.1.call-start = ((), (), s32[]{:S(2)}) async-start(), calls=%async_computation.34 | async-start | bytes 1179648 | tf_op jit(solution)/shard_map/reduce_scatter | solution.py:269
  (217 other events, 6294.1 us)
Sparse Core Ops, SparseCore 0:
  10.5 28.5 all-gather.3
  113.4 104.7 reduce-scatter.22
  246.9 100.0 reduce-scatter.26
  376.6 78.2 reduce-scatter.30
  456.8 27.2 all-gather.5
  486.0 27.8 all-gather.7
  551.5 139.7 reduce-scatter.38
  714.5 137.8 reduce-scatter.34
  854.8 82.1 reduce-scatter.28
  939.1 77.2 reduce-scatter.24
  1018.9 77.2 reduce-scatter.42
  1098.3 77.2 reduce-scatter.32
  1275.6 114.6 reduce-scatter.44
  1392.5 78.0 reduce-scatter.40
  1472.9 77.2 reduce-scatter.36
  1554.0 46.7 reduce-scatter.46
  1604.0 34.0 reduce-scatter.54
  1641.1 34.0 reduce-scatter.56
  1679.5 51.3 reduce-scatter.52
  1734.6 51.2 reduce-scatter.50
  1790.0 36.0 reduce-scatter.48
